TPU v7x, 32 devices: a whole 2x2x4 slice. The times are simulated.
32 devices in a mesh: fsdp: 8 (over y, x, core), tp: 4 (over z).
Axes of the slice: x: 2, y: 2, z: 4, core: 2. Of those that a mesh axis runs over, the one named last changes fastest.
Arguments:
- hidden_in: bfloat16 [4096, 2048], P(('fsdp', 'tp')), may hold values from -6 to 6
- cotangent: bfloat16 [4096, 2048], P(('fsdp', 'tp')), may hold values from -6 to 6
- seq_lengths: int32 [8, 4], P('fsdp'), may hold values from 1 to 256, 512 in all within a row
- attn_gain: bfloat16 [2048], P('fsdp'), may hold values from 0.5 to 1.5
- w_query: bfloat16 [2048, 2048], P('fsdp', 'tp'), may hold values from -0.125 to 0.125
- key_weight: bfloat16 [2048, 1024], P('fsdp', 'tp'), may hold values from -0.125 to 0.125
- value_weight: bfloat16 [2048, 1024], P('fsdp', 'tp'), may hold values from -0.125 to 0.125
- q_gain: bfloat16 [128], P('fsdp'), may hold values from 0.5 to 1.5
- k_gain: bfloat16 [128], P('fsdp'), may hold values from 0.5 to 1.5
- w_out: bfloat16 [2048, 2048], P('tp', 'fsdp'), may hold values from -0.5 to 0.5
- mlp_gain: bfloat16 [2048], P('fsdp'), may hold values from 0.5 to 1.5
- w_gate: bfloat16 [2048, 6144], P('fsdp', 'tp'), may hold values from -0.125 to 0.125
- w_up: bfloat16 [2048, 6144], P('fsdp', 'tp'), may hold values from -0.125 to 0.125
- w_down: bfloat16 [6144, 2048], P('tp', 'fsdp'), may hold values from -0.15625 to 0.15625
Outputs:
- block_out: bfloat16 [4096, 2048], P(('fsdp', 'tp'))
- grad_in: bfloat16 [4096, 2048], P(('fsdp', 'tp'))
- grad_attn_gain: float32 [2048], P('fsdp')
- grad_query: float32 [2048, 2048], P('fsdp', 'tp')
- grad_key: float32 [2048, 1024], P('fsdp', 'tp')
- grad_value: float32 [2048, 1024], P('fsdp', 'tp')
- grad_q_gain: float32 [128], P('fsdp')
- grad_k_gain: float32 [128], P('fsdp')
- grad_out_proj: float32 [2048, 2048], P('tp', 'fsdp')
- grad_mlp_gain: float32 [2048], P('fsdp')
- grad_gate: float32 [2048, 6144], P('fsdp', 'tp')
- grad_up: float32 [2048, 6144], P('fsdp', 'tp')
- grad_down: float32 [6144, 2048], P('tp', 'fsdp')
Inputs may be any that keep to these rules, and one draw needn't show every extreme that they name: `seq_lengths`: row s holds the lengths of the sequences packed, in order, in data shard s; each row sums to 512 and its largest entry is exactly 256.
All inputs are finite; a program needn't handle non-finite values.
Results may differ from a plain program's by a relative error of at most 0.025.
Values may be sent and summed in bfloat16 or wider, within the bound.
No kernel may reach another device: no remote copies, remote signals or barrier semaphores. Data moves between devices by JAX's collectives and lax.ppermute only.
A program may use at most 192 MiB of HBM per device.

v0:
```python
import math
import jax
import jax.numpy as jnp
from jax import lax
from jax.sharding import PartitionSpec as P

EPS = 1e-06
THETA = 1000000.0


def positions(lens_row, row_count):
    seq_ends = jnp.cumsum(lens_row)
    token_index = jnp.arange(row_count, dtype=jnp.int32)
    finished = token_index[:, None] >= seq_ends[None, :]
    seq_start = jnp.sum(jnp.where(finished, lens_row[None, :], 0), axis=1)
    return (token_index, seq_start)


def rope_tables(offset, head_width):
    half_width = head_width // 2
    frequency = jnp.exp(
        jnp.arange(half_width, dtype=jnp.float32) * (-2.0 * math.log(THETA) / head_width)
    )
    phase_angle = offset.astype(jnp.float32)[:, None] * frequency[None, :]
    return (jnp.cos(phase_angle)[:, None, :], jnp.sin(phase_angle)[:, None, :])


def rotate(values, cosine, sine):
    half_width = values.shape[-1] // 2
    first_half, second_half = (values[..., :half_width], values[..., half_width:])
    return jnp.concatenate(
        [first_half * cosine - second_half * sine, second_half * cosine + first_half * sine],
        axis=-1,
    )


def unrotate(values, cosine, sine):
    half_width = values.shape[-1] // 2
    first_half, second_half = (values[..., :half_width], values[..., half_width:])
    return jnp.concatenate(
        [first_half * cosine + second_half * sine, second_half * cosine - first_half * sine],
        axis=-1,
    )


def row_norm(values, gain_vec):
    inv_rms = lax.rsqrt(jnp.mean(values * values, axis=-1, keepdims=True) + EPS)
    normed = values * inv_rms
    return (normed * gain_vec.astype(jnp.float32), normed, inv_rms)


def norm_back(incoming, normed, inv_rms, gain_vec):
    scaled = incoming * gain_vec.astype(jnp.float32)
    grad_back = inv_rms * (scaled - normed * jnp.mean(scaled * normed, axis=-1, keepdims=True))
    gain_grad = jnp.sum((incoming * normed).reshape(-1, incoming.shape[-1]), axis=0)
    return (grad_back, gain_grad)


def attend(query_rot, key_rot, value, token_index, seq_start, score_scale):
    row_count, head_count, head_width = query_rot.shape
    kv_heads = key_rot.shape[1]
    groups = head_count // kv_heads
    block_rows = min(512, row_count)
    block_count = row_count // block_rows
    query_block_list = query_rot.reshape(block_count, block_rows, kv_heads, groups, head_width)

    def block_step(block_in):
        query_block, query_pos, query_start = block_in
        scores = (
            jnp.einsum("bkgd,skd->kgbs", query_block, key_rot, preferred_element_type=jnp.float32)
            * score_scale
        )
        allowed = (token_index[None, :] <= query_pos[:, None]) & (
            token_index[None, :] >= query_start[:, None]
        )
        scores = jnp.where(allowed, scores, -1e30)
        row_max = jnp.max(scores, axis=-1, keepdims=True)
        exp_scores = jnp.exp(scores - row_max)
        row_total = jnp.sum(exp_scores, axis=-1, keepdims=True)
        prob_bf = (exp_scores / row_total).astype(jnp.bfloat16)
        block_out = jnp.einsum("kgbs,skd->bkgd", prob_bf, value, preferred_element_type=jnp.float32)
        return (block_out.astype(jnp.bfloat16), (row_max + jnp.log(row_total))[..., 0])

    block_outs, log_sums = lax.map(
        block_step,
        (
            query_block_list,
            token_index.reshape(block_count, block_rows),
            seq_start.reshape(block_count, block_rows),
        ),
    )
    return (block_outs.reshape(row_count, head_count, head_width), log_sums)


def attend_back(
    query_rot, key_rot, value, attended, d_attended, log_sums, token_index, seq_start, score_scale
):
    row_count, head_count, head_width = query_rot.shape
    kv_heads = key_rot.shape[1]
    groups = head_count // kv_heads
    block_rows = min(512, row_count)
    block_count = row_count // block_rows
    shaped = (block_count, block_rows, kv_heads, groups, head_width)

    def block_step(totals, block_in):
        key_grad, value_grad = totals
        query_block, out_block, dout_block, lse_block, query_pos, query_start = block_in
        scores = (
            jnp.einsum("bkgd,skd->kgbs", query_block, key_rot, preferred_element_type=jnp.float32)
            * score_scale
        )
        allowed = (token_index[None, :] <= query_pos[:, None]) & (
            token_index[None, :] >= query_start[:, None]
        )
        probs = jnp.where(allowed, jnp.exp(scores - lse_block[..., None]), 0.0)
        prob_bf = probs.astype(jnp.bfloat16)
        value_grad = value_grad + jnp.einsum(
            "kgbs,bkgd->skd", prob_bf, dout_block, preferred_element_type=jnp.float32
        )
        d_prob = jnp.einsum("bkgd,skd->kgbs", dout_block, value, preferred_element_type=jnp.float32)
        row_delta = jnp.transpose(
            jnp.sum(dout_block.astype(jnp.float32) * out_block.astype(jnp.float32), axis=-1),
            (1, 2, 0),
        )
        d_score = (probs * (d_prob - row_delta[..., None]) * score_scale).astype(jnp.bfloat16)
        query_grad = jnp.einsum(
            "kgbs,skd->bkgd", d_score, key_rot, preferred_element_type=jnp.float32
        )
        key_grad = key_grad + jnp.einsum(
            "kgbs,bkgd->skd", d_score, query_block, preferred_element_type=jnp.float32
        )
        return ((key_grad, value_grad), query_grad)

    empty_kv = jnp.zeros((row_count, kv_heads, head_width), jnp.float32)
    block_in = (
        query_rot.reshape(shaped),
        attended.reshape(shaped),
        d_attended.reshape(shaped),
        log_sums,
        token_index.reshape(block_count, block_rows),
        seq_start.reshape(block_count, block_rows),
    )
    (key_grad, value_grad), query_grads = lax.scan(block_step, (empty_kv, empty_kv), block_in)
    return (query_grads.reshape(row_count, head_count, head_width), key_grad, value_grad)


def local(
    hidden_in,
    cotangent,
    seq_lengths,
    attn_gain,
    w_query,
    key_weight,
    value_weight,
    q_gain,
    k_gain,
    w_out,
    mlp_gain,
    w_gate,
    w_up,
    w_down,
):
    gain_attn, wq_full, wk_full, wv_full, gain_query, gain_key, wo_full = (
        lax.all_gather(attn_gain, "fsdp", axis=0, tiled=True),
        lax.all_gather(w_query, "fsdp", axis=0, tiled=True),
        lax.all_gather(key_weight, "fsdp", axis=0, tiled=True),
        lax.all_gather(value_weight, "fsdp", axis=0, tiled=True),
        lax.all_gather(q_gain, "fsdp", axis=0, tiled=True),
        lax.all_gather(k_gain, "fsdp", axis=0, tiled=True),
        lax.all_gather(w_out, "fsdp", axis=1, tiled=True),
    )
    feedforward_gain, wg_full, wu_full, wd_full = (
        lax.all_gather(mlp_gain, "fsdp", axis=0, tiled=True),
        lax.all_gather(w_gate, "fsdp", axis=0, tiled=True),
        lax.all_gather(w_up, "fsdp", axis=0, tiled=True),
        lax.all_gather(w_down, "fsdp", axis=1, tiled=True),
    )
    head_width = gain_query.shape[0]
    score_scale = 1.0 / math.sqrt(head_width)
    x_float = hidden_in.astype(jnp.float32)
    normed_in, hat_in, inv_in = row_norm(x_float, gain_attn)
    attn_in = lax.all_gather(normed_in.astype(jnp.bfloat16), "tp", axis=0, tiled=True)
    row_count = attn_in.shape[0]
    token_index, seq_start = positions(seq_lengths[0], row_count)
    cosine, sine = rope_tables(token_index - seq_start, head_width)
    query = jnp.dot(attn_in, wq_full, preferred_element_type=jnp.float32).reshape(
        row_count, -1, head_width
    )
    key_proj = jnp.dot(attn_in, wk_full, preferred_element_type=jnp.float32).reshape(
        row_count, -1, head_width
    )
    value = (
        jnp.dot(attn_in, wv_full, preferred_element_type=jnp.float32)
        .astype(jnp.bfloat16)
        .reshape(row_count, -1, head_width)
    )
    q_scaled, q_hat, q_inv = row_norm(query, gain_query)
    k_scaled, k_hat, k_inv = row_norm(key_proj, gain_key)
    query_rot = rotate(q_scaled, cosine, sine).astype(jnp.bfloat16)
    key_rot = rotate(k_scaled, cosine, sine).astype(jnp.bfloat16)
    attended, log_sums = attend(query_rot, key_rot, value, token_index, seq_start, score_scale)
    attended_flat = attended.reshape(row_count, -1)
    residual = x_float + lax.psum_scatter(
        jnp.dot(attended_flat, wo_full, preferred_element_type=jnp.float32),
        "tp",
        scatter_dimension=0,
        tiled=True,
    )
    normed_mid, hat_mid, inv_mid = row_norm(residual, feedforward_gain)
    mlp_in = lax.all_gather(normed_mid.astype(jnp.bfloat16), "tp", axis=0, tiled=True)
    gate_act = jnp.dot(mlp_in, wg_full, preferred_element_type=jnp.float32)
    up_act = jnp.dot(mlp_in, wu_full, preferred_element_type=jnp.float32)
    sigmoid_gate = 1.0 / (1.0 + jnp.exp(-gate_act))
    hidden = (gate_act * sigmoid_gate * up_act).astype(jnp.bfloat16)
    block_out = (
        residual
        + lax.psum_scatter(
            jnp.dot(hidden, wd_full, preferred_element_type=jnp.float32).astype(jnp.bfloat16),
            "tp",
            scatter_dimension=0,
            tiled=True,
        ).astype(jnp.float32)
    ).astype(jnp.bfloat16)
    grad_all = lax.all_gather(cotangent, "tp", axis=0, tiled=True)
    grad_down = jnp.dot(hidden.T, grad_all, preferred_element_type=jnp.float32)
    d_hidden = jnp.dot(grad_all, wd_full.T, preferred_element_type=jnp.float32)
    d_gate = (d_hidden * up_act * sigmoid_gate * (1.0 + gate_act * (1.0 - sigmoid_gate))).astype(
        jnp.bfloat16
    )
    d_up = (d_hidden * gate_act * sigmoid_gate).astype(jnp.bfloat16)
    grad_gate = jnp.dot(mlp_in.T, d_gate, preferred_element_type=jnp.float32)
    grad_up = jnp.dot(mlp_in.T, d_up, preferred_element_type=jnp.float32)
    d_mlp_in = lax.psum_scatter(
        (
            jnp.dot(d_gate, wg_full.T, preferred_element_type=jnp.float32)
            + jnp.dot(d_up, wu_full.T, preferred_element_type=jnp.float32)
        ).astype(jnp.bfloat16),
        "tp",
        scatter_dimension=0,
        tiled=True,
    ).astype(jnp.float32)
    d_mid, grad_gain_mlp = norm_back(d_mlp_in, hat_mid, inv_mid, feedforward_gain)
    d_residual = cotangent.astype(jnp.float32) + d_mid
    d_attn = lax.all_gather(d_residual.astype(jnp.bfloat16), "tp", axis=0, tiled=True)
    grad_out_proj = jnp.dot(attended_flat.T, d_attn, preferred_element_type=jnp.float32)
    d_attended = (
        jnp.dot(d_attn, wo_full.T, preferred_element_type=jnp.float32)
        .astype(jnp.bfloat16)
        .reshape(row_count, -1, head_width)
    )
    dq_rot, dk_rot, d_value = attend_back(
        query_rot,
        key_rot,
        value,
        attended,
        d_attended,
        log_sums,
        token_index,
        seq_start,
        score_scale,
    )
    d_query, grad_gain_query = norm_back(unrotate(dq_rot, cosine, sine), q_hat, q_inv, gain_query)
    d_key, grad_gain_key = norm_back(unrotate(dk_rot, cosine, sine), k_hat, k_inv, gain_key)
    d_query_bf = d_query.reshape(row_count, -1).astype(jnp.bfloat16)
    d_key_bf = d_key.reshape(row_count, -1).astype(jnp.bfloat16)
    d_value_bf = d_value.reshape(row_count, -1).astype(jnp.bfloat16)
    grad_query = jnp.dot(attn_in.T, d_query_bf, preferred_element_type=jnp.float32)
    grad_key = jnp.dot(attn_in.T, d_key_bf, preferred_element_type=jnp.float32)
    grad_value = jnp.dot(attn_in.T, d_value_bf, preferred_element_type=jnp.float32)
    d_attn_in = lax.psum_scatter(
        (
            jnp.dot(d_query_bf, wq_full.T, preferred_element_type=jnp.float32)
            + jnp.dot(d_key_bf, wk_full.T, preferred_element_type=jnp.float32)
            + jnp.dot(d_value_bf, wv_full.T, preferred_element_type=jnp.float32)
        ).astype(jnp.bfloat16),
        "tp",
        scatter_dimension=0,
        tiled=True,
    ).astype(jnp.float32)
    d_in_norm, grad_gain_attn = norm_back(d_attn_in, hat_in, inv_in, gain_attn)
    grad_in = (d_residual + d_in_norm).astype(jnp.bfloat16)
    every_sum = (
        lax.psum_scatter(
            grad_gain_attn.astype(jnp.bfloat16), "fsdp", scatter_dimension=0, tiled=True
        ).astype(jnp.float32),
        lax.psum_scatter(
            grad_query.astype(jnp.bfloat16), "fsdp", scatter_dimension=0, tiled=True
        ).astype(jnp.float32),
        lax.psum_scatter(
            grad_key.astype(jnp.bfloat16), "fsdp", scatter_dimension=0, tiled=True
        ).astype(jnp.float32),
        lax.psum_scatter(
            grad_value.astype(jnp.bfloat16), "fsdp", scatter_dimension=0, tiled=True
        ).astype(jnp.float32),
        lax.psum_scatter(
            grad_gain_query.astype(jnp.bfloat16), "fsdp", scatter_dimension=0, tiled=True
        ).astype(jnp.float32),
        lax.psum_scatter(
            grad_gain_key.astype(jnp.bfloat16), "fsdp", scatter_dimension=0, tiled=True
        ).astype(jnp.float32),
        lax.psum_scatter(
            grad_out_proj.astype(jnp.bfloat16), "fsdp", scatter_dimension=1, tiled=True
        ).astype(jnp.float32),
        lax.psum_scatter(
            grad_gain_mlp.astype(jnp.bfloat16), "fsdp", scatter_dimension=0, tiled=True
        ).astype(jnp.float32),
        lax.psum_scatter(
            grad_gate.astype(jnp.bfloat16), "fsdp", scatter_dimension=0, tiled=True
        ).astype(jnp.float32),
        lax.psum_scatter(
            grad_up.astype(jnp.bfloat16), "fsdp", scatter_dimension=0, tiled=True
        ).astype(jnp.float32),
        lax.psum_scatter(
            grad_down.astype(jnp.bfloat16), "fsdp", scatter_dimension=1, tiled=True
        ).astype(jnp.float32),
    )
    attn_sums = every_sum[:7]
    mlp_sums = every_sum[7:]
    gain_totals = lax.psum((attn_sums[0], attn_sums[4], attn_sums[5], mlp_sums[0]), "tp")
    return (
        block_out,
        grad_in,
        gain_totals[0],
        attn_sums[1],
        attn_sums[2],
        attn_sums[3],
        gain_totals[1],
        gain_totals[2],
        attn_sums[6],
        gain_totals[3],
        mlp_sums[1],
        mlp_sums[2],
        mlp_sums[3],
    )


def solution(mesh):
    return jax.shard_map(
        local,
        mesh=mesh,
        in_specs=(
            P(("fsdp", "tp"), None),
            P(("fsdp", "tp"), None),
            P("fsdp", None),
            P("fsdp"),
            P("fsdp", "tp"),
            P("fsdp", "tp"),
            P("fsdp", "tp"),
            P("fsdp"),
            P("fsdp"),
            P("tp", "fsdp"),
            P("fsdp"),
            P("fsdp", "tp"),
            P("fsdp", "tp"),
            P("tp", "fsdp"),
        ),
        out_specs=(
            P(("fsdp", "tp"), None),
            P(("fsdp", "tp"), None),
            P("fsdp"),
            P("fsdp", "tp"),
            P("fsdp", "tp"),
            P("fsdp", "tp"),
            P("fsdp"),
            P("fsdp"),
            P("tp", "fsdp"),
            P("fsdp"),
            P("fsdp", "tp"),
            P("fsdp", "tp"),
            P("tp", "fsdp"),
        ),
        check_vma=False,
    )
```

profile of v0, /device:TPU:0, one launch (start us, length us, event | category | flops | bytes accessed | tf_op | source)
XLA Modules:
  0.0 1075.7 jit_solution(12785175896997641999)
XLA Ops:
  8.7 10.4 all-gather
  27.8 13.5 %all-reduce.8 = (bf16[128]{0:T(256)(128)(2,1)S(1)}, bf16[128]{0:T(256)(128)(2,1)S(1)}) all-reduce(bf16[128]{0:T(256)(128)(2,1)S(1)} %dynamic-update-slice.1, bf16[128]{0:T(256)(128)(2,1)S(1)} %dynamic-update-slice), channel_id=1, replica_groups=mesh['fsdp'=8,'tp'=4] {'fsdp'}, use_global_device_ids=true, to_apply=%add.1 | all-reduce | flops 256 | bytes 1024
  42.3 41.6 %all-gather.14.cloned.1.call-done = bf16[512,2048]{1,0:T(8,128)(2,1)} async-done(((bf16[128,2048]{1,0:T(8,128)(2,1)}), bf16[512,2048]{1,0:T(8,128)(2,1)}) %all-gather.14.cloned.1.call-update) | async-done | bytes 2097168 | tf_op jit(solution)/shard_map/all_gather | solution.py:182
  84.0 2.6 multiply_reduce_fusion.5
  88.1 20.0 %all-gather.16.cloned.1.call-done = bf16[2048,256]{1,0:T(8,128)(2,1)} async-done(((bf16[256,256]{1,0:T(8,128)(2,1)}), bf16[2048,256]{1,0:T(8,128)(2,1)}) %all-gather.16.cloned.1.call-update) | async-done | bytes 1048592 | tf_op jit(solution)/shard_map/all_gather | solution.py:167
  108.1 3.3 convolution_convert_fusion.9
  111.4 26.2 %all-gather.20.cloned.1.call-done = bf16[2048,512]{1,0:T(8,128)(2,1)} async-done(((bf16[256,512]{1,0:T(8,128)(2,1)}), bf16[2048,512]{1,0:T(8,128)(2,1)}) %all-gather.20.cloned.1.call-update) | async-done | bytes 2097168 | tf_op jit(solution)/shard_map/all_gather | solution.py:165
  137.6 3.5 multiply_reduce_fusion.3
  148.4 19.1 %all-gather.22.cloned.1.call-done = bf16[512,2048]{1,0:T(8,128)(2,1)} async-done(((bf16[512,256]{1,0:T(8,128)(2,1)}), bf16[512,2048]{1,0:T(8,128)(2,1)}) %all-gather.22.cloned.1.call-update) | async-done | bytes 2097168 | tf_op jit(solution)/shard_map/all_gather | solution.py:170
  167.5 4.8 fusion.58
  173.2 8.9 all-gather.1
  182.1 67.2 %reduce-scatter.12.cloned.1.call-done = f32[128,2048]{1,0:T(8,128)} async-done(((f32[512,2048]{1,0:T(8,128)}), f32[128,2048]{1,0:T(8,128)}) %reduce-scatter.12.cloned.1.call-update) | async-done | bytes 1048592 | tf_op jit(solution)/shard_map/reduce_scatter | solution.py:203
  254.0 43.1 %all-gather.26.cloned.1.call-done = bf16[2048,1536]{1,0:T(8,128)(2,1)} async-done(((bf16[256,1536]{1,0:T(8,128)(2,1)}), bf16[2048,1536]{1,0:T(8,128)(2,1)}) %all-gather.26.cloned.1.call-update) | async-done | bytes 6291472 | tf_op jit(solution)/shard_map/all_gather | solution.py:174
  297.1 47.8 %all-gather.24.cloned.1.call-done = bf16[512,2048]{1,0:T(8,128)(2,1)} async-done(((bf16[128,2048]{1,0:T(8,128)(2,1)}), bf16[512,2048]{1,0:T(8,128)(2,1)}) %all-gather.24.cloned.1.call-update) | async-done | bytes 2097168 | tf_op jit(solution)/shard_map/all_gather | solution.py:210
  344.9 8.5 fusion.59
  353.5 37.6 %all-gather.28.cloned.1.call-done = bf16[2048,1536]{1,0:T(8,128)(2,1)} async-done(((bf16[256,1536]{1,0:T(8,128)(2,1)}), bf16[2048,1536]{1,0:T(8,128)(2,1)}) %all-gather.28.cloned.1.call-update) | async-done | bytes 6291472 | tf_op jit(solution)/shard_map/all_gather | solution.py:175
  391.1 8.6 fusion.60
  399.6 38.5 %all-gather.32.cloned.1.call-done = bf16[512,2048]{1,0:T(8,128)(2,1)} async-done(((bf16[128,2048]{1,0:T(8,128)(2,1)}), bf16[512,2048]{1,0:T(8,128)(2,1)}) %all-gather.32.cloned.1.call-update) | async-done | bytes 2097168 | tf_op jit(solution)/shard_map/all_gather | solution.py:224
  438.2 47.3 %all-gather.30.cloned.1.call-done = bf16[1536,2048]{1,0:T(8,128)(2,1)} async-done(((bf16[1536,256]{1,0:T(8,128)(2,1)}), bf16[1536,2048]{1,0:T(8,128)(2,1)}) %all-gather.30.cloned.1.call-update) | async-done | bytes 6291472 | tf_op jit(solution)/shard_map/all_gather | solution.py:176
  485.5 11.0 %multiply_convert_fusion = (bf16[512,1536]{1,0:T(8,128)(2,1)S(1)}, bf16[512,1536]{1,0:T(8,128)(2,1)S(1)}, bf16[512,1536]{1,0:T(8,128)(2,1)}) fusion(f32[512,1536]{1,0:T(8,128)} %fusion.59, f32[512,1536]{1,0:T(8,128)} %fusion.60, bf16[512,2048]{1,0:T(8,128)(2,1)} %all-gather.32.cloned.1.call-done, bf16[1536,2048]{1,0:T(8,128)(2,1)} %all-gather.30.cloned.1.call-done), kind=kOutput, calls=%fused_computation.18 | convolution fusion | flops 3233808384 | bytes 19398656 | tf_op jit(solution)/shard_map/dot_general | solution.py:226
  496.4 6.7 fusion.61
  503.2 4.8 add_convert_fusion.1
  508.1 43.7 %reduce-scatter.16.cloned.1.call-done = bf16[128,2048]{1,0:T(8,128)(2,1)} async-done(((bf16[512,2048]{1,0:T(8,128)(2,1)}), bf16[128,2048]{1,0:T(8,128)(2,1)}) %reduce-scatter.16.cloned.1.call-update) | async-done | bytes 524304 | tf_op jit(solution)/shard_map/reduce_scatter | solution.py:233
  555.9 44.7 %all-gather.34.cloned.1.call-done = bf16[512,2048]{1,0:T(8,128)(2,1)} async-done(((bf16[128,2048]{1,0:T(8,128)(2,1)}), bf16[512,2048]{1,0:T(8,128)(2,1)}) %all-gather.34.cloned.1.call-update) | async-done | bytes 2097168 | tf_op jit(solution)/shard_map/all_gather | solution.py:244
  600.6 3.8 multiply_reduce_fusion.1
  613.6 3.3 convolution_convert_fusion.7
  617.1 3.5 fusion.23
  623.2 8.3 convolution_convert_fusion.2
  631.9 8.1 convolution_convert_fusion.1
  640.1 8.2 convolution_convert_fusion
  659.5 3.6 multiply_reduce_fusion
  667.3 4.4 convolution_convert_fusion.4
  671.9 4.2 convolution_convert_fusion.3
  679.9 2.7 add_convert_fusion
  682.7 8.0 convolution_convert_fusion.5
  698.5 2.6 reshape.257
  708.7 47.3 %reduce-scatter.28.cloned.1.call-done = bf16[256,1536]{1,0:T(8,128)(2,1)} async-done(((bf16[2048,1536]{1,0:T(8,128)(2,1)}), bf16[256,1536]{1,0:T(8,128)(2,1)}) %reduce-scatter.28.cloned.1.call-update) | async-done | bytes 786448 | tf_op jit(solution)/shard_map/reduce_scatter | solution.py:307
  756.0 2.5 convert_element_type.240
  758.4 62.6 %reduce-scatter.30.cloned.1.call-done = bf16[256,1536]{1,0:T(8,128)(2,1)} async-done(((bf16[2048,1536]{1,0:T(8,128)(2,1)}), bf16[256,1536]{1,0:T(8,128)(2,1)}) %reduce-scatter.30.cloned.1.call-update) | async-done | bytes 786448 | tf_op jit(solution)/shard_map/reduce_scatter | solution.py:310
  821.0 2.5 convert_element_type.242
  823.5 62.4 %reduce-scatter.32.cloned.1.call-done = bf16[1536,256]{1,0:T(8,128)(2,1)} async-done(((bf16[1536,2048]{1,0:T(8,128)(2,1)}), bf16[1536,256]{1,0:T(8,128)(2,1)}) %reduce-scatter.32.cloned.1.call-update) | async-done | bytes 786448 | tf_op jit(solution)/shard_map/reduce_scatter | solution.py:313
  888.2 42.0 %reduce-scatter.20.cloned.1.call-done = bf16[256,512]{1,0:T(8,128)(2,1)} async-done(((bf16[2048,512]{1,0:T(8,128)(2,1)}), bf16[256,512]{1,0:T(8,128)(2,1)}) %reduce-scatter.20.cloned.1.call-update) | async-done | bytes 262160 | tf_op jit(solution)/shard_map/reduce_scatter | solution.py:286
  932.1 42.5 %reduce-scatter.26.cloned.1.call-done = bf16[512,256]{1,0:T(8,128)(2,1)} async-done(((bf16[512,2048]{1,0:T(8,128)(2,1)}), bf16[512,256]{1,0:T(8,128)(2,1)}) %reduce-scatter.26.cloned.1.call-update) | async-done | bytes 262160 | tf_op jit(solution)/shard_map/reduce_scatter | solution.py:301
  976.3 44.2 %reduce-scatter.18.cloned.1.call-done = bf16[128,2048]{1,0:T(8,128)(2,1)} async-done(((bf16[512,2048]{1,0:T(8,128)(2,1)}), bf16[128,2048]{1,0:T(8,128)(2,1)}) %reduce-scatter.18.cloned.1.call-update) | async-done | bytes 524304 | tf_op jit(solution)/shard_map/reduce_scatter | solution.py:270
  1022.0 13.8 %all-reduce.7 = (bf16[2048]{0:T(1024)(128)(2,1)S(1)}, bf16[128]{0:T(256)(128)(2,1)S(1)}, bf16[128]{0:T(256)(128)(2,1)S(1)}, bf16[2048]{0:T(1024)(128)(2,1)S(1)}) all-reduce(bf16[2048]{0:T(1024)(128)(2,1)S(1)} %get-tuple-element.68, bf16[128]{0:T(256)(128)(2,1)S(1)} %fusion.40, ...), channel_id=6, replica_groups=mesh['fsdp'=8,'tp'=4] {'fsdp'}, use_global_device_ids=true, to_apply=%region_18.19.clone | all-reduce | flops 4352 | bytes 17408
  1035.9 11.8 %all-reduce.6 = (f32[256]{0:T(256)}, f32[16]{0:T(128)}, f32[16]{0:T(128)}, f32[256]{0:T(256)}) all-reduce(f32[256]{0:T(256)S(1)} %get-tuple-element.127, f32[16]{0:T(128)S(1)} %get-tuple-element.129, f32[16]{0:T(128)S(1)} %get-tuple-element.128, f32[256]{0:T(256)S(1)} %get-tuple-element.126), channel_id=1, replica_groups=mesh['fsdp'=8,'tp'=4] {'tp'}, use_global_device_ids=true, to_apply=%region_19.20 | all-reduce | flops 544 | bytes 4352 | tf_op jit(solution)/shard_map/psum | solution.py:319
  1047.8 18.1 %reduce-scatter.14.cloned.1.call-done = bf16[128,2048]{1,0:T(8,128)(2,1)} async-done(((bf16[512,2048]{1,0:T(8,128)(2,1)}), bf16[128,2048]{1,0:T(8,128)(2,1)}) %reduce-scatter.14.cloned.1.call-update) | async-done | bytes 524304 | tf_op jit(solution)/shard_map/reduce_scatter | solution.py:217
  1065.9 2.7 fusion.28
  (227 shorter events, 81.6 us)
Async XLA Ops:
  7.2 18.9 %copy-start.37 = (u32[32]{0:T(128)S(1)}, u32[32]{0:T(128)}, u32[]{:S(2)}) copy-start(u32[32]{0:T(128)} %constant.76) | copy-start | bytes 388
  7.2 20.2 %copy-start.39 = (bf16[16]{0:T(256)(128)(2,1)S(1)}, bf16[16]{0:T(256)(128)(2,1)}, u32[]{:S(2)}) copy-start(bf16[16]{0:T(256)(128)(2,1)} %param.22) | copy-start | bytes 100
  7.2 20.4 %copy-start.40 = (bf16[16]{0:T(256)(128)(2,1)S(1)}, bf16[16]{0:T(256)(128)(2,1)}, u32[]{:S(2)}) copy-start(bf16[16]{0:T(256)(128)(2,1)} %param.21) | copy-start | bytes 100
  7.2 35.1 %all-gather.18.cloned.1.call-start = ((), (), s32[]{:S(2)}) async-start(), calls=%async_computation.13 | async-start | bytes 1179648 | tf_op jit(solution)/shard_map/all_gather | solution.py:166
  7.9 76.0 %all-gather.14.cloned.1.call-start = ((), (), s32[]{:S(2)}) async-start(), calls=%async_computation.11 | async-start | bytes 2621440 | tf_op jit(solution)/shard_map/all_gather | solution.py:182
  22.4 85.7 %all-gather.16.cloned.1.call-start = ((), (), s32[]{:S(2)}) async-start(), calls=%async_computation.12 | async-start | bytes 1179648 | tf_op jit(solution)/shard_map/all_gather | solution.py:167
  23.1 114.5 %all-gather.20.cloned.1.call-start = ((), (), s32[]{:S(2)}) async-start(), calls=%async_computation.14 | async-start | bytes 2359296 | tf_op jit(solution)/shard_map/all_gather | solution.py:165
  23.7 143.8 %all-gather.22.cloned.1.call-start = ((), (), s32[]{:S(2)}) async-start(), calls=%async_computation.15 | async-start | bytes 2359296 | tf_op jit(solution)/shard_map/all_gather | solution.py:170
  24.3 225.0 %reduce-scatter.12.cloned.1.call-start = ((), (), s32[]{:S(2)}) async-start(), calls=%async_computation.16 | async-start | bytes 5242880 | tf_op jit(solution)/shard_map/reduce_scatter | solution.py:203
  86.6 24.8 %copy-start.21 = (f32[512,256]{0,1:T(8,128)}, f32[512,256]{0,1:T(8,128)S(1)}, u32[]{:S(2)}) copy-start(f32[512,256]{0,1:T(8,128)S(1)} %get-tuple-element.121) | copy-start | bytes 1572868
  86.8 24.6 %copy-start.19 = (f32[512,2,128]{2,0,1:T(8,128)}, f32[512,2,128]{2,0,1:T(8,128)S(1)}, u32[]{:S(2)}) copy-start(f32[512,2,128]{2,0,1:T(8,128)S(1)} %copy.122) | copy-start | bytes 1572868
  148.4 19.1 %copy-start.35 = (bf16[2,128,2,512]{3,1,2,0:T(8,128)(2,1)}, bf16[2,128,2,512]{3,1,2,0:T(8,128)(2,1)S(1)}, u32[]{:S(2)}) copy-start(bf16[2,128,2,512]{3,1,2,0:T(8,128)(2,1)S(1)} %fusion.16) | copy-start | bytes 1572868
  172.3 77.0 %copy-start.2 = (bf16[128,2048]{1,0:T(8,128)(2,1)S(1)}, bf16[128,2048]{1,0:T(8,128)(2,1)}, u32[]{:S(2)}) copy-start(bf16[128,2048]{1,0:T(8,128)(2,1)} %param.14) | copy-start | bytes 1572868
  172.4 124.8 %all-gather.26.cloned.1.call-start = ((), (), s32[]{:S(2)}) async-start(), calls=%async_computation.18 | async-start | bytes 7077888 | tf_op jit(solution)/shard_map/all_gather | solution.py:174
  173.1 171.8 %all-gather.24.cloned.1.call-start = ((), (), s32[]{:S(2)}) async-start(), calls=%async_computation.17 | async-start | bytes 2621440 | tf_op jit(solution)/shard_map/all_gather | solution.py:210
  251.7 139.3 %all-gather.28.cloned.1.call-start = ((), (), s32[]{:S(2)}) async-start(), calls=%async_computation.19 | async-start | bytes 7077888 | tf_op jit(solution)/shard_map/all_gather | solution.py:175
  252.5 185.7 %all-gather.32.cloned.1.call-start = ((), (), s32[]{:S(2)}) async-start(), calls=%async_computation.22 | async-start | bytes 2621440 | tf_op jit(solution)/shard_map/all_gather | solution.py:224
  253.1 232.4 %all-gather.30.cloned.1.call-start = ((), (), s32[]{:S(2)}) async-start(), calls=%async_computation.20 | async-start | bytes 7077888 | tf_op jit(solution)/shard_map/all_gather | solution.py:176
  253.8 298.0 %reduce-scatter.16.cloned.1.call-start = ((), (), s32[]{:S(2)}) async-start(), calls=%async_computation.23 | async-start | bytes 2621440 | tf_op jit(solution)/shard_map/reduce_scatter | solution.py:233
  485.5 17.8 %slice-start = ((s8[6291456]{0:T(1024)(128)(4,1)}), s8[2097152]{0:T(1024)(128)(4,1)S(1)}, s32[]{:S(2)}) async-start(s8[6291456]{0:T(1024)(128)(4,1)} %bitcast.204), calls=%async_computation.33 | async-start | bytes 4194304
  496.4 6.8 copy-start.46
  496.4 6.8 copy-start.45
  496.4 6.8 slice-start.1
  508.0 92.6 %all-gather.34.cloned.1.call-start = ((), (), s32[]{:S(2)}) async-start(), calls=%async_computation.24 | async-start | bytes 2621440 | tf_op jit(solution)/shard_map/all_gather | solution.py:244
  555.6 149.8 %reduce-scatter.22.cloned.1.call-start = ((), (), s32[]{:S(2)}) async-start(), calls=%async_computation.27 | async-start | bytes 1179648 | tf_op jit(solution)/shard_map/reduce_scatter | solution.py:289
  600.6 3.8 copy-start.1
  600.6 3.8 copy-start.44
  617.0 90.0 %reduce-scatter.24.cloned.1.call-start = ((), (), s32[]{:S(2)}) async-start(), calls=%async_computation.28 | async-start | bytes 1179648 | tf_op jit(solution)/shard_map/reduce_scatter | solution.py:292
  617.1 4.3 copy-start.38
  623.1 132.9 %reduce-scatter.28.cloned.1.call-start = ((), (), s32[]{:S(2)}) async-start(), calls=%async_computation.30 | async-start | bytes 7077888 | tf_op jit(solution)/shard_map/reduce_scatter | solution.py:307
  631.5 189.5 %reduce-scatter.30.cloned.1.call-start = ((), (), s32[]{:S(2)}) async-start(), calls=%async_computation.31 | async-start | bytes 7077888 | tf_op jit(solution)/shard_map/reduce_scatter | solution.py:310
  640.1 245.8 %reduce-scatter.32.cloned.1.call-start = ((), (), s32[]{:S(2)}) async-start(), calls=%async_computation.32 | async-start | bytes 7077888 | tf_op jit(solution)/shard_map/reduce_scatter | solution.py:313
  648.4 281.9 %reduce-scatter.20.cloned.1.call-start = ((), (), s32[]{:S(2)}) async-start(), calls=%async_computation.26 | async-start | bytes 2359296 | tf_op jit(solution)/shard_map/reduce_scatter | solution.py:286
  655.0 4.5 copy-start.24
  659.5 3.7 copy-start.5
  659.5 3.6 copy-start.7
  667.3 4.6 copy-start.36
  671.7 4.5 copy-start.31
  671.7 302.8 %reduce-scatter.26.cloned.1.call-start = ((), (), s32[]{:S(2)}) async-start(), calls=%async_computation.29 | async-start | bytes 2359296 | tf_op jit(solution)/shard_map/reduce_scatter | solution.py:301
  676.2 344.3 %reduce-scatter.18.cloned.1.call-start = ((), (), s32[]{:S(2)}) async-start(), calls=%async_computation.25 | async-start | bytes 2621440 | tf_op jit(solution)/shard_map/reduce_scatter | solution.py:270
  682.7 10.4 copy-start.22
  682.7 383.2 %reduce-scatter.14.cloned.1.call-start = ((), (), s32[]{:S(2)}) async-start(), calls=%async_computation.21 | async-start | bytes 2621440 | tf_op jit(solution)/shard_map/reduce_scatter | solution.py:217
  690.8 6.5 copy-start.4
  695.1 7.7 copy-start.12
  698.5 6.2 copy-start.6
  701.2 3.6 copy-start.25
  758.4 307.5 %copy-start.10 = (bf16[128,2048]{1,0:T(8,128)(2,1)S(1)}, bf16[128,2048]{1,0:T(8,128)(2,1)}, u32[]{:S(2)}) copy-start(bf16[128,2048]{1,0:T(8,128)(2,1)} %param.15) | copy-start | bytes 1572868
  758.4 307.5 %copy-start.18 = (bf16[128,2048]{1,0:T(8,128)(2,1)S(1)}, bf16[128,2048]{1,0:T(8,128)(2,1)}, u32[]{:S(2)}) copy-start(bf16[128,2048]{1,0:T(8,128)(2,1)} %reduce-scatter.16.cloned.1.call-done) | copy-start | bytes 1572868
  (23 other events, 37.0 us)
Sparse Core Ops, SparseCore 0:
  9.9 26.1 all-gather.17
  38.2 45.6 all-gather.13
  85.9 22.1 all-gather.15
  109.8 27.7 all-gather.19
  139.3 28.0 all-gather.21
  172.5 76.7 reduce-scatter.11
  251.2 45.8 all-gather.25
  299.2 45.6 all-gather.23
  346.8 44.1 all-gather.27
  392.5 45.6 all-gather.31
  440.0 45.3 all-gather.29
  508.1 43.5 reduce-scatter.15
  555.7 44.8 all-gather.33
  617.1 34.7 reduce-scatter.21
  654.9 35.9 reduce-scatter.23
  694.2 61.7 reduce-scatter.27
  759.2 61.7 reduce-scatter.29
  824.2 61.5 reduce-scatter.31
  889.1 41.0 reduce-scatter.19
  933.4 41.0 reduce-scatter.25
  976.8 43.6 reduce-scatter.17
  1022.8 43.0 reduce-scatter.13
where the time goes:
time: 1090 us; the launch traced here: 1080 us
  waiting for transfers between devices  801 us (73%)
  matrix products  121 us (11%)
  blocking collectives  58.4 us (5%)
  other arithmetic  46.5 us (4%)
  local copies, waits for them, and re-layouts  29.7 us (3%)
  between operations  17.4 us (2%)
    reduce_scatter x1, waiting for transfers between devices, local(): lax.psum_scatter(jnp.dot(attended_flat, wo_full, preferred_element_type=j...  67.2 us
    reduce_scatter x1, waiting for transfers between devices, local(): lax.psum_scatter(grad_up.astype(jnp.bfloat16), 'fsdp', scatter_dimension=...  62.6 us
    reduce_scatter x1, waiting for transfers between devices, local(): lax.psum_scatter(grad_down.astype(jnp.bfloat16), 'fsdp', scatter_dimensio...  62.4 us
    all_gather x1, waiting for transfers between devices, local(): lax.all_gather(normed_mid.astype(jnp.bfloat16), 'tp', axis=0, tiled=True)  47.8 us
    all_gather x1, waiting for transfers between devices, local(): lax.all_gather(w_down, 'fsdp', axis=1, tiled=True)  47.3 us
    reduce_scatter x1, waiting for transfers between devices, local(): lax.psum_scatter(grad_gate.astype(jnp.bfloat16), 'fsdp', scatter_dimensio...  47.3 us
    all_gather x1, waiting for transfers between devices, local(): lax.all_gather(d_residual.astype(jnp.bfloat16), 'tp', axis=0, tiled=True)  44.7 us
    reduce_scatter x1, waiting for transfers between devices, local(): lax.psum_scatter((jnp.dot(d_query_bf, wq_full.T, preferred_element_type=j...  44.2 us
  transfers between devices with their start and end apart: 22, of which 19 were waited for; matrix products, arithmetic and copies ran while one was open for 13% of the time, Pallas kernels for 0%

commit v1 on v0

--- a/solution.py
+++ b/solution.py
@@ -207,7 +207,12 @@
         tiled=True,
     )
     normed_mid, hat_mid, inv_mid = row_norm(residual, feedforward_gain)
-    mlp_in = lax.all_gather(normed_mid.astype(jnp.bfloat16), "tp", axis=0, tiled=True)
+    mlp_in = jnp.concatenate(
+        lax.all_to_all(
+            jnp.stack([normed_mid.astype(jnp.bfloat16)] * lax.axis_size("tp")), "tp", 0, 0
+        ),
+        axis=0,
+    )
     gate_act = jnp.dot(mlp_in, wg_full, preferred_element_type=jnp.float32)
     up_act = jnp.dot(mlp_in, wu_full, preferred_element_type=jnp.float32)
     sigmoid_gate = 1.0 / (1.0 + jnp.exp(-gate_act))

time: 1090 us -> 1040 us (0.954)
  waiting for transfers between devices: 801 us -> 751 us
    all_gather x1 -> x0, waiting for transfers between devices: 47.8 us -> none  [local(): lax.all_gather(normed_mid.astype(jnp.bfloat16), 'tp', axis=0, tiled=True)]
  transfers between devices with their start and end apart: 22 -> 22, of which waited for: 19 -> 19; matrix products, arithmetic and copies ran while one was open for 13% -> 14% of each run, Pallas kernels for 0% -> 0%
where the time goes in v1:
time: 1040 us; the launch traced here: 1030 us
  waiting for transfers between devices  751 us (72%)
  matrix products  121 us (12%)
  blocking collectives  58.3 us (6%)
  other arithmetic  45.1 us (4%)
  local copies, waits for them, and re-layouts  30.1 us (3%)
  between operations  17.4 us (2%)
    reduce_scatter x1, waiting for transfers between devices, local(): lax.psum_scatter(jnp.dot(attended_flat, wo_full, preferred_element_type=j...  65.2 us
    reduce_scatter x1, waiting for transfers between devices, local(): lax.psum_scatter(grad_up.astype(jnp.bfloat16), 'fsdp', scatter_dimension=...  62.6 us
    reduce_scatter x1, waiting for transfers between devices, local(): lax.psum_scatter(grad_down.astype(jnp.bfloat16), 'fsdp', scatter_dimensio...  62.4 us
    reduce_scatter x1, waiting for transfers between devices, local(): lax.psum_scatter(grad_gate.astype(jnp.bfloat16), 'fsdp', scatter_dimensio...  49.2 us
    all_gather x1, waiting for transfers between devices, local(): lax.all_gather(w_down, 'fsdp', axis=1, tiled=True)  47.1 us
    all_gather x1, waiting for transfers between devices, local(): lax.all_gather(d_residual.astype(jnp.bfloat16), 'tp', axis=0, tiled=True)  44.7 us
    reduce_scatter x1, waiting for transfers between devices, local(): lax.psum_scatter((jnp.dot(d_query_bf, wq_full.T, preferred_element_type=j...  44 us
    reduce_scatter x1, waiting for transfers between devices, local(): lax.psum_scatter((jnp.dot(d_gate, wg_full.T, preferred_element_type=jnp.f...  43.7 us
  transfers between devices with their start and end apart: 22, of which 19 were waited for; matrix products, arithmetic and copies ran while one was open for 14% of the time, Pallas kernels for 0%

profile of v1, /device:TPU:0, one launch (start us, length us, event | category | flops | bytes accessed | tf_op | source)
XLA Modules:
  0.0 1029.1 jit_solution(8437211736208437760)
XLA Ops:
  8.7 10.4 %all-gather = bf16[8,1,256]{2,1,0:T(2,128)(2,1)S(1)} all-gather(bf16[1,1,256]{2,1,0:T(2,128)(2,1)S(1)} %reshape.271), channel_id=1, replica_groups=mesh['fsdp'=8,'tp'=4] {'fsdp'}, dimensions={0}, use_global_device_ids=true | all-gather | bytes 4608 | tf_op jit(solution)/shard_map/all_gather | solution.py:164
  27.8 13.5 %all-reduce.8 = (bf16[128]{0:T(256)(128)(2,1)S(1)}, bf16[128]{0:T(256)(128)(2,1)S(1)}) all-reduce(bf16[128]{0:T(256)(128)(2,1)S(1)} %dynamic-update-slice.1, bf16[128]{0:T(256)(128)(2,1)S(1)} %dynamic-update-slice), channel_id=1, replica_groups=mesh['fsdp'=8,'tp'=4] {'fsdp'}, use_global_device_ids=true, to_apply=%add.1 | all-reduce | flops 256 | bytes 1024
  42.3 41.6 %all-gather.13.cloned.1.call-done = bf16[512,2048]{1,0:T(8,128)(2,1)} async-done(((bf16[128,2048]{1,0:T(8,128)(2,1)}), bf16[512,2048]{1,0:T(8,128)(2,1)}) %all-gather.13.cloned.1.call-update) | async-done | bytes 2097168 | tf_op jit(solution)/shard_map/all_gather | solution.py:182
  84.0 2.6 multiply_reduce_fusion.5
  88.1 20.0 %all-gather.15.cloned.1.call-done = bf16[2048,256]{1,0:T(8,128)(2,1)} async-done(((bf16[256,256]{1,0:T(8,128)(2,1)}), bf16[2048,256]{1,0:T(8,128)(2,1)}) %all-gather.15.cloned.1.call-update) | async-done | bytes 1048592 | tf_op jit(solution)/shard_map/all_gather | solution.py:167
  108.1 3.3 convolution_convert_fusion.9
  111.4 26.2 %all-gather.19.cloned.1.call-done = bf16[2048,512]{1,0:T(8,128)(2,1)} async-done(((bf16[256,512]{1,0:T(8,128)(2,1)}), bf16[2048,512]{1,0:T(8,128)(2,1)}) %all-gather.19.cloned.1.call-update) | async-done | bytes 2097168 | tf_op jit(solution)/shard_map/all_gather | solution.py:165
  137.6 3.5 multiply_reduce_fusion.3
  148.4 19.1 %all-gather.21.cloned.1.call-done = bf16[512,2048]{1,0:T(8,128)(2,1)} async-done(((bf16[512,256]{1,0:T(8,128)(2,1)}), bf16[512,2048]{1,0:T(8,128)(2,1)}) %all-gather.21.cloned.1.call-update) | async-done | bytes 2097168 | tf_op jit(solution)/shard_map/all_gather | solution.py:170
  167.5 4.9 fusion.58
  175.3 8.9 all-gather.1
  184.2 65.2 %reduce-scatter.12.cloned.1.call-done = f32[128,2048]{1,0:T(8,128)} async-done(((f32[512,2048]{1,0:T(8,128)}), f32[128,2048]{1,0:T(8,128)}) %reduce-scatter.12.cloned.1.call-update) | async-done | bytes 1048592 | tf_op jit(solution)/shard_map/reduce_scatter | solution.py:203
  252.7 4.4 all-to-all-start
  257.4 39.8 %all-gather.23.cloned.1.call-done = bf16[2048,1536]{1,0:T(8,128)(2,1)} async-done(((bf16[256,1536]{1,0:T(8,128)(2,1)}), bf16[2048,1536]{1,0:T(8,128)(2,1)}) %all-gather.23.cloned.1.call-update) | async-done | bytes 6291472 | tf_op jit(solution)/shard_map/all_gather | solution.py:174
  297.2 8.7 all-to-all-done
  305.9 9.0 fusion.59
  314.9 29.6 %all-gather.25.cloned.1.call-done = bf16[2048,1536]{1,0:T(8,128)(2,1)} async-done(((bf16[256,1536]{1,0:T(8,128)(2,1)}), bf16[2048,1536]{1,0:T(8,128)(2,1)}) %all-gather.25.cloned.1.call-update) | async-done | bytes 6291472 | tf_op jit(solution)/shard_map/all_gather | solution.py:175
  344.5 8.6 fusion.60
  353.1 38.7 %all-gather.29.cloned.1.call-done = bf16[512,2048]{1,0:T(8,128)(2,1)} async-done(((bf16[128,2048]{1,0:T(8,128)(2,1)}), bf16[512,2048]{1,0:T(8,128)(2,1)}) %all-gather.29.cloned.1.call-update) | async-done | bytes 2097168 | tf_op jit(solution)/shard_map/all_gather | solution.py:229
  391.8 47.1 %all-gather.27.cloned.1.call-done = bf16[1536,2048]{1,0:T(8,128)(2,1)} async-done(((bf16[1536,256]{1,0:T(8,128)(2,1)}), bf16[1536,2048]{1,0:T(8,128)(2,1)}) %all-gather.27.cloned.1.call-update) | async-done | bytes 6291472 | tf_op jit(solution)/shard_map/all_gather | solution.py:176
  438.9 11.0 %multiply_convert_fusion = (bf16[512,1536]{1,0:T(8,128)(2,1)S(1)}, bf16[512,1536]{1,0:T(8,128)(2,1)S(1)}, bf16[512,1536]{1,0:T(8,128)(2,1)}) fusion(f32[512,1536]{1,0:T(8,128)} %fusion.59, f32[512,1536]{1,0:T(8,128)} %fusion.60, bf16[512,2048]{1,0:T(8,128)(2,1)} %all-gather.29.cloned.1.call-done, bf16[1536,2048]{1,0:T(8,128)(2,1)} %all-gather.27.cloned.1.call-done), kind=kOutput, calls=%fused_computation.18 | convolution fusion | flops 3233808384 | bytes 19398656 | tf_op jit(solution)/shard_map/dot_general | solution.py:231
  449.9 6.7 fusion.61
  456.7 4.8 add_convert_fusion.1
  461.5 43.7 %reduce-scatter.16.cloned.1.call-done = bf16[128,2048]{1,0:T(8,128)(2,1)} async-done(((bf16[512,2048]{1,0:T(8,128)(2,1)}), bf16[128,2048]{1,0:T(8,128)(2,1)}) %reduce-scatter.16.cloned.1.call-update) | async-done | bytes 524304 | tf_op jit(solution)/shard_map/reduce_scatter | solution.py:238
  509.4 44.7 %all-gather.31.cloned.1.call-done = bf16[512,2048]{1,0:T(8,128)(2,1)} async-done(((bf16[128,2048]{1,0:T(8,128)(2,1)}), bf16[512,2048]{1,0:T(8,128)(2,1)}) %all-gather.31.cloned.1.call-update) | async-done | bytes 2097168 | tf_op jit(solution)/shard_map/all_gather | solution.py:249
  554.1 3.7 multiply_reduce_fusion.1
  567.1 3.4 convolution_convert_fusion.7
  570.6 3.5 fusion.23
  576.7 8.3 convolution_convert_fusion.2
  585.5 8.1 convolution_convert_fusion.1
  593.7 8.2 convolution_convert_fusion
  613.0 2.9 multiply_reduce_fusion
  619.2 4.4 convolution_convert_fusion.4
  623.9 4.2 convolution_convert_fusion.3
  631.9 2.7 add_convert_fusion
  634.7 8.0 convolution_convert_fusion.5
  660.4 49.2 %reduce-scatter.28.cloned.1.call-done = bf16[256,1536]{1,0:T(8,128)(2,1)} async-done(((bf16[2048,1536]{1,0:T(8,128)(2,1)}), bf16[256,1536]{1,0:T(8,128)(2,1)}) %reduce-scatter.28.cloned.1.call-update) | async-done | bytes 786448 | tf_op jit(solution)/shard_map/reduce_scatter | solution.py:312
  709.5 2.5 convert_element_type.240
  712.0 62.6 %reduce-scatter.30.cloned.1.call-done = bf16[256,1536]{1,0:T(8,128)(2,1)} async-done(((bf16[2048,1536]{1,0:T(8,128)(2,1)}), bf16[256,1536]{1,0:T(8,128)(2,1)}) %reduce-scatter.30.cloned.1.call-update) | async-done | bytes 786448 | tf_op jit(solution)/shard_map/reduce_scatter | solution.py:315
  774.5 2.5 convert_element_type.242
  777.0 62.4 %reduce-scatter.32.cloned.1.call-done = bf16[1536,256]{1,0:T(8,128)(2,1)} async-done(((bf16[1536,2048]{1,0:T(8,128)(2,1)}), bf16[1536,256]{1,0:T(8,128)(2,1)}) %reduce-scatter.32.cloned.1.call-update) | async-done | bytes 786448 | tf_op jit(solution)/shard_map/reduce_scatter | solution.py:318
  841.8 41.9 %reduce-scatter.20.cloned.1.call-done = bf16[256,512]{1,0:T(8,128)(2,1)} async-done(((bf16[2048,512]{1,0:T(8,128)(2,1)}), bf16[256,512]{1,0:T(8,128)(2,1)}) %reduce-scatter.20.cloned.1.call-update) | async-done | bytes 262160 | tf_op jit(solution)/shard_map/reduce_scatter | solution.py:291
  885.5 42.6 %reduce-scatter.26.cloned.1.call-done = bf16[512,256]{1,0:T(8,128)(2,1)} async-done(((bf16[512,2048]{1,0:T(8,128)(2,1)}), bf16[512,256]{1,0:T(8,128)(2,1)}) %reduce-scatter.26.cloned.1.call-update) | async-done | bytes 262160 | tf_op jit(solution)/shard_map/reduce_scatter | solution.py:306
  929.9 44.0 %reduce-scatter.18.cloned.1.call-done = bf16[128,2048]{1,0:T(8,128)(2,1)} async-done(((bf16[512,2048]{1,0:T(8,128)(2,1)}), bf16[128,2048]{1,0:T(8,128)(2,1)}) %reduce-scatter.18.cloned.1.call-update) | async-done | bytes 524304 | tf_op jit(solution)/shard_map/reduce_scatter | solution.py:275
  975.4 13.8 %all-reduce.7 = (bf16[2048]{0:T(1024)(128)(2,1)S(1)}, bf16[128]{0:T(256)(128)(2,1)S(1)}, bf16[128]{0:T(256)(128)(2,1)S(1)}, bf16[2048]{0:T(1024)(128)(2,1)S(1)}) all-reduce(bf16[2048]{0:T(1024)(128)(2,1)S(1)} %get-tuple-element.68, bf16[128]{0:T(256)(128)(2,1)S(1)} %fusion.40, ...), channel_id=6, replica_groups=mesh['fsdp'=8,'tp'=4] {'fsdp'}, use_global_device_ids=true, to_apply=%region_18.19.clone | all-reduce | flops 4352 | bytes 17408
  989.3 11.8 %all-reduce.6 = (f32[256]{0:T(256)}, f32[16]{0:T(128)}, f32[16]{0:T(128)}, f32[256]{0:T(256)}) all-reduce(f32[256]{0:T(256)S(1)} %get-tuple-element.127, f32[16]{0:T(128)S(1)} %get-tuple-element.129, f32[16]{0:T(128)S(1)} %get-tuple-element.128, f32[256]{0:T(256)S(1)} %get-tuple-element.126), channel_id=1, replica_groups=mesh['fsdp'=8,'tp'=4] {'tp'}, use_global_device_ids=true, to_apply=%region_19.20 | all-reduce | flops 544 | bytes 4352 | tf_op jit(solution)/shard_map/psum | solution.py:324
  1001.1 18.2 %reduce-scatter.14.cloned.1.call-done = bf16[128,2048]{1,0:T(8,128)(2,1)} async-done(((bf16[512,2048]{1,0:T(8,128)(2,1)}), bf16[128,2048]{1,0:T(8,128)(2,1)}) %reduce-scatter.14.cloned.1.call-update) | async-done | bytes 524304 | tf_op jit(solution)/shard_map/reduce_scatter | solution.py:222
  1019.3 2.7 fusion.28
  (227 shorter events, 83.8 us)
Async XLA Ops:
  7.2 18.9 %copy-start.37 = (u32[32]{0:T(128)S(1)}, u32[32]{0:T(128)}, u32[]{:S(2)}) copy-start(u32[32]{0:T(128)} %constant.76) | copy-start | bytes 388
  7.2 20.2 %copy-start.39 = (bf16[16]{0:T(256)(128)(2,1)S(1)}, bf16[16]{0:T(256)(128)(2,1)}, u32[]{:S(2)}) copy-start(bf16[16]{0:T(256)(128)(2,1)} %param.22) | copy-start | bytes 100
  7.2 20.4 %copy-start.40 = (bf16[16]{0:T(256)(128)(2,1)S(1)}, bf16[16]{0:T(256)(128)(2,1)}, u32[]{:S(2)}) copy-start(bf16[16]{0:T(256)(128)(2,1)} %param.21) | copy-start | bytes 100
  7.2 35.1 %all-gather.17.cloned.1.call-start = ((), (), s32[]{:S(2)}) async-start(), calls=%async_computation.14 | async-start | bytes 1179648 | tf_op jit(solution)/shard_map/all_gather | solution.py:166
  7.9 76.0 %all-gather.13.cloned.1.call-start = ((), (), s32[]{:S(2)}) async-start(), calls=%async_computation.12 | async-start | bytes 2621440 | tf_op jit(solution)/shard_map/all_gather | solution.py:182
  22.4 85.7 %all-gather.15.cloned.1.call-start = ((), (), s32[]{:S(2)}) async-start(), calls=%async_computation.13 | async-start | bytes 1179648 | tf_op jit(solution)/shard_map/all_gather | solution.py:167
  23.1 114.5 %all-gather.19.cloned.1.call-start = ((), (), s32[]{:S(2)}) async-start(), calls=%async_computation.15 | async-start | bytes 2359296 | tf_op jit(solution)/shard_map/all_gather | solution.py:165
  23.7 143.8 %all-gather.21.cloned.1.call-start = ((), (), s32[]{:S(2)}) async-start(), calls=%async_computation.16 | async-start | bytes 2359296 | tf_op jit(solution)/shard_map/all_gather | solution.py:170
  24.3 225.1 %reduce-scatter.12.cloned.1.call-start = ((), (), s32[]{:S(2)}) async-start(), calls=%async_computation.17 | async-start | bytes 5242880 | tf_op jit(solution)/shard_map/reduce_scatter | solution.py:203
  86.6 24.8 %copy-start.21 = (f32[512,256]{0,1:T(8,128)}, f32[512,256]{0,1:T(8,128)S(1)}, u32[]{:S(2)}) copy-start(f32[512,256]{0,1:T(8,128)S(1)} %get-tuple-element.121) | copy-start | bytes 1572868
  86.8 24.6 %copy-start.19 = (f32[512,2,128]{2,0,1:T(8,128)}, f32[512,2,128]{2,0,1:T(8,128)S(1)}, u32[]{:S(2)}) copy-start(f32[512,2,128]{2,0,1:T(8,128)S(1)} %copy.122) | copy-start | bytes 1572868
  148.4 24.0 %copy-start.35 = (bf16[2,128,2,512]{3,1,2,0:T(8,128)(2,1)}, bf16[2,128,2,512]{3,1,2,0:T(8,128)(2,1)S(1)}, u32[]{:S(2)}) copy-start(bf16[2,128,2,512]{3,1,2,0:T(8,128)(2,1)S(1)} %fusion.16) | copy-start | bytes 1572868
  172.4 77.0 %copy-start.2 = (bf16[128,2048]{1,0:T(8,128)(2,1)S(1)}, bf16[128,2048]{1,0:T(8,128)(2,1)}, u32[]{:S(2)}) copy-start(bf16[128,2048]{1,0:T(8,128)(2,1)} %param.14) | copy-start | bytes 1572868
  172.4 124.8 %all-gather.23.cloned.1.call-start = ((), (), s32[]{:S(2)}) async-start(), calls=%async_computation.18 | async-start | bytes 7077888 | tf_op jit(solution)/shard_map/all_gather | solution.py:174
  173.2 171.3 %all-gather.25.cloned.1.call-start = ((), (), s32[]{:S(2)}) async-start(), calls=%async_computation.19 | async-start | bytes 7077888 | tf_op jit(solution)/shard_map/all_gather | solution.py:175
  173.9 217.8 %all-gather.29.cloned.1.call-start = ((), (), s32[]{:S(2)}) async-start(), calls=%async_computation.22 | async-start | bytes 2621440 | tf_op jit(solution)/shard_map/all_gather | solution.py:229
  174.7 264.2 %all-gather.27.cloned.1.call-start = ((), (), s32[]{:S(2)}) async-start(), calls=%async_computation.20 | async-start | bytes 7077888 | tf_op jit(solution)/shard_map/all_gather | solution.py:176
  252.7 53.2 %all-to-all-start = ((bf16[4,128,2048]{2,1,0:T(8,128)(2,1)}), bf16[4,128,2048]{2,1,0:T(8,128)(2,1)}, u32[]{:S(2)}, u32[]{:S(2)}) async-start(bf16[4,128,2048]{2,1,0:T(8,128)(2,1)} %stack.2), calls=%async_computation.1 | async-start | bytes 4194304 | tf_op jit(solution)/shard_map/all_to_all | solution.py:211
  257.1 248.1 %reduce-scatter.16.cloned.1.call-start = ((), (), s32[]{:S(2)}) async-start(), calls=%async_computation.23 | async-start | bytes 2621440 | tf_op jit(solution)/shard_map/reduce_scatter | solution.py:238
  438.9 17.8 %slice-start = ((s8[6291456]{0:T(1024)(128)(4,1)}), s8[2097152]{0:T(1024)(128)(4,1)S(1)}, s32[]{:S(2)}) async-start(s8[6291456]{0:T(1024)(128)(4,1)} %bitcast.205), calls=%async_computation.33 | async-start | bytes 4194304
  449.9 6.8 copy-start.46
  449.9 6.8 copy-start.45
  449.9 6.8 slice-start.1
  461.5 92.6 %all-gather.31.cloned.1.call-start = ((), (), s32[]{:S(2)}) async-start(), calls=%async_computation.24 | async-start | bytes 2621440 | tf_op jit(solution)/shard_map/all_gather | solution.py:249
  509.1 148.0 %reduce-scatter.22.cloned.1.call-start = ((), (), s32[]{:S(2)}) async-start(), calls=%async_computation.27 | async-start | bytes 1179648 | tf_op jit(solution)/shard_map/reduce_scatter | solution.py:294
  554.1 3.8 copy-start.1
  554.1 3.8 copy-start.44
  570.5 88.2 %reduce-scatter.24.cloned.1.call-start = ((), (), s32[]{:S(2)}) async-start(), calls=%async_computation.28 | async-start | bytes 1179648 | tf_op jit(solution)/shard_map/reduce_scatter | solution.py:297
  570.6 4.3 copy-start.38
  576.6 132.9 %reduce-scatter.28.cloned.1.call-start = ((), (), s32[]{:S(2)}) async-start(), calls=%async_computation.30 | async-start | bytes 7077888 | tf_op jit(solution)/shard_map/reduce_scatter | solution.py:312
  585.0 189.5 %reduce-scatter.30.cloned.1.call-start = ((), (), s32[]{:S(2)}) async-start(), calls=%async_computation.31 | async-start | bytes 7077888 | tf_op jit(solution)/shard_map/reduce_scatter | solution.py:315
  593.6 245.8 %reduce-scatter.32.cloned.1.call-start = ((), (), s32[]{:S(2)}) async-start(), calls=%async_computation.32 | async-start | bytes 7077888 | tf_op jit(solution)/shard_map/reduce_scatter | solution.py:318
  601.9 281.8 %reduce-scatter.20.cloned.1.call-start = ((), (), s32[]{:S(2)}) async-start(), calls=%async_computation.26 | async-start | bytes 2359296 | tf_op jit(solution)/shard_map/reduce_scatter | solution.py:291
  608.5 4.5 copy-start.24
  613.0 3.0 copy-start.5
  619.2 4.7 copy-start.36
  623.6 4.5 copy-start.31
  623.6 304.5 %reduce-scatter.26.cloned.1.call-start = ((), (), s32[]{:S(2)}) async-start(), calls=%async_computation.29 | async-start | bytes 2359296 | tf_op jit(solution)/shard_map/reduce_scatter | solution.py:306
  628.1 345.8 %reduce-scatter.18.cloned.1.call-start = ((), (), s32[]{:S(2)}) async-start(), calls=%async_computation.25 | async-start | bytes 2621440 | tf_op jit(solution)/shard_map/reduce_scatter | solution.py:275
  634.6 10.3 %copy-start.22 = (f32[512,256]{0,1:T(8,128)S(1)}, f32[512,256]{0,1:T(8,128)}, u32[]{:S(2)}) copy-start(f32[512,256]{0,1:T(8,128)} %copy-done.21) | copy-start | bytes 1572868
  634.6 384.7 %reduce-scatter.14.cloned.1.call-start = ((), (), s32[]{:S(2)}) async-start(), calls=%async_computation.21 | async-start | bytes 2621440 | tf_op jit(solution)/shard_map/reduce_scatter | solution.py:222
  642.7 6.5 copy-start.4
  647.1 7.4 copy-start.12
  650.5 5.9 copy-start.6
  652.8 3.6 copy-start.8
  652.8 3.6 copy-start.25
  712.0 307.3 %copy-start.10 = (bf16[128,2048]{1,0:T(8,128)(2,1)S(1)}, bf16[128,2048]{1,0:T(8,128)(2,1)}, u32[]{:S(2)}) copy-start(bf16[128,2048]{1,0:T(8,128)(2,1)} %param.15) | copy-start | bytes 1572868
  712.0 307.3 %copy-start.18 = (bf16[128,2048]{1,0:T(8,128)(2,1)S(1)}, bf16[128,2048]{1,0:T(8,128)(2,1)}, u32[]{:S(2)}) copy-start(bf16[128,2048]{1,0:T(8,128)(2,1)} %reduce-scatter.16.cloned.1.call-done) | copy-start | bytes 1572868
  (23 other events, 38.5 us)
Sparse Core Ops, SparseCore 0:
  9.9 26.1 all-gather.16
  38.2 45.6 all-gather.12
  85.9 22.1 all-gather.14
  109.8 27.7 all-gather.18
  139.3 28.0 all-gather.20
  172.6 76.7 reduce-scatter.11
  251.3 45.8 all-gather.22
  299.1 45.3 all-gather.24
  346.1 45.6 all-gather.28
  393.5 45.3 all-gather.26
  461.6 43.6 reduce-scatter.15
  509.2 44.8 all-gather.30
  570.6 34.8 reduce-scatter.21
  608.5 35.9 reduce-scatter.23
  647.7 61.7 reduce-scatter.27
  712.8 61.7 reduce-scatter.29
  777.8 61.5 reduce-scatter.31
  842.5 41.1 reduce-scatter.19
  887.0 41.0 reduce-scatter.25
  930.2 43.5 reduce-scatter.17
  976.2 43.0 reduce-scatter.13
